TPU v7x, 32 devices: a whole 2x2x4 slice. The times are simulated.
32 devices in a mesh: corpus: 4 (over y, x), fsdp: 8 (over z, core).
Axes of the slice: x: 2, y: 2, z: 4, core: 2. Of those that a mesh axis runs over, the one named last changes fastest.
Arguments:
- inputs: bfloat16 [2048, 4096], P('fsdp', 'corpus'), may hold values from -128 to 128
- norm_gain: float32 [4096], replicated, may hold values from 0.1 to 1.9
- w_query: bfloat16 [4096, 8192], P('fsdp', 'corpus'), may hold values from -0.09375 to 0.09375
- w_key: bfloat16 [4096, 1024], P('fsdp', 'corpus'), may hold values from -0.09375 to 0.09375
- w_value: bfloat16 [4096, 1024], P('fsdp', 'corpus'), may hold values from -0.375 to 0.375
- query_bias: float32 [8192], P('corpus'), may hold values from -16 to 16
- key_bias: float32 [1024], P('corpus'), may hold values from -16 to 16
- value_bias: float32 [1024], P('corpus'), may hold values from -4 to 4
- key_cache: bfloat16 [8, 2048, 1024], P('fsdp', None, 'corpus'), may hold values from -16 to 16
- value_cache: bfloat16 [8, 2048, 1024], P('fsdp', None, 'corpus'), may hold values from -16 to 16
- source_doc: int32 [32], P('fsdp'), may hold values from 0 to 7, as said below
- prefix_len: int32 [32], P('fsdp'), may hold values from 1 to 2048
Outputs:
- attention: bfloat16 [2048, 8192], P('fsdp', 'corpus')
Inputs may be any that keep to these rules, and one draw needn't show every extreme that they name: `source_doc`: within the suffixes of one index of fsdp (aligned blocks of 4) no document appears more than 2 times, and one document, drawn from the seed, appears exactly 2 times in every such block.
All inputs are finite; a program needn't handle non-finite values.
Results may differ from a plain program's by a relative error of at most 0.0075.
The roundings to bfloat16 on the way count: a program that leaves them out, or rounds other values in their place, can miss the bound.
Values may be sent and summed in bfloat16 or wider, within the bound.
A program may use at most 128 MiB of HBM per device.

v0:
```python
import jax
import jax.numpy as jnp
from jax import lax
from jax.sharding import PartitionSpec as P

HD = 128
SL = 64
CAP = 2
EPS = 1e-06
THETA = 1000000.0
MASKED = -1e30


def rope_tables(position, width):
    half = width // 2
    freq = THETA ** (-(jnp.arange(half, dtype=jnp.float32) * 2.0 / width))
    angle = position.astype(jnp.float32)[..., None] * freq
    angle = jnp.concatenate([angle, angle], axis=-1)
    return (jnp.cos(angle), jnp.sin(angle))


def rotate(vector, cosine, sine):
    half = vector.shape[-1] // 2
    turned = jnp.concatenate([-vector[..., half:], vector[..., :half]], axis=-1)
    return vector * cosine + turned * sine


def normalize(rows, norm_gain):
    wide = rows.astype(jnp.float32)
    spread = jnp.mean(wide * wide, axis=-1, keepdims=True)
    return (wide * lax.rsqrt(spread + EPS) * norm_gain).astype(jnp.bfloat16)


def partial_attend(query, keys, values, live):
    count = query.shape[0]
    width = query.shape[2]
    length = keys.shape[0]
    kv_heads = keys.shape[1] // width
    group = query.shape[1] // kv_heads
    grouped = query.reshape(count, kv_heads, group, width)
    key_rows = keys.reshape(length, kv_heads, width)
    scores = jnp.einsum(
        "tkgd,lkd->tkgl", grouped, key_rows, preferred_element_type=jnp.float32
    ) * width ** (-0.5)
    scores = jnp.where(live[:, None, None, :], scores, MASKED)
    peak = jnp.max(scores, axis=-1)
    weights = jnp.exp(scores - peak[..., None])
    total = jnp.sum(weights, axis=-1)
    rounded = weights.astype(jnp.bfloat16)
    value_rows = values.reshape(length, kv_heads, width)
    weighted = jnp.einsum("tkgl,lkd->tkgd", rounded, value_rows, preferred_element_type=jnp.float32)
    return (
        weighted.reshape(count, kv_heads * group * width),
        peak.reshape(count, kv_heads * group),
        total.reshape(count, kv_heads * group),
    )


def settle(part):
    weighted, peak, total = part
    shape = peak.shape + (-1,)
    normed = (
        (weighted.reshape(shape) / total[..., None]).reshape(weighted.shape).astype(jnp.bfloat16)
    )
    return (normed, peak + jnp.log(total))


def combine(prefix_normed, prefix_lse, own):
    own_out, own_peak, own_total = own
    top = jnp.maximum(prefix_lse, own_peak)
    scale_first = jnp.exp(prefix_lse - top)
    scale_second = jnp.exp(own_peak - top)
    divisor = scale_first + own_total * scale_second
    shape = own_peak.shape + (-1,)
    mixed = (
        prefix_normed.astype(jnp.float32).reshape(shape) * scale_first[..., None]
        + own_out.reshape(shape) * scale_second[..., None]
    )
    mixed = mixed / divisor[..., None]
    return mixed.reshape(own_peak.shape[:-1] + (-1,)).astype(jnp.bfloat16)


def shards(
    inputs,
    norm_gain,
    w_query,
    w_key,
    w_value,
    query_bias,
    key_bias,
    value_bias,
    key_cache,
    value_cache,
    source_doc,
    prefix_len,
):
    full_rows = lax.all_gather(inputs, "corpus", axis=1, tiled=True)
    normed = normalize(full_rows, norm_gain)
    query_lin = jnp.dot(
        normed,
        lax.all_gather(w_query, "fsdp", axis=0, tiled=True),
        preferred_element_type=jnp.float32,
    )
    key_lin = jnp.dot(
        normed,
        lax.all_gather(w_key, "fsdp", axis=0, tiled=True),
        preferred_element_type=jnp.float32,
    )
    value_lin = jnp.dot(
        normed,
        lax.all_gather(w_value, "fsdp", axis=0, tiled=True),
        preferred_element_type=jnp.float32,
    )
    suffixes = source_doc.shape[0]
    width = HD
    q_heads = w_query.shape[1] // width
    kv_heads = w_key.shape[1] // width
    position = prefix_len[:, None] + jnp.arange(SL, dtype=jnp.int32)[None, :]
    cosine, sine = rope_tables(position, width)
    cosine = cosine[:, :, None, :]
    sine = sine[:, :, None, :]
    queries = rotate(
        (query_lin + query_bias).reshape(suffixes, SL, q_heads, width), cosine, sine
    ).astype(jnp.bfloat16)
    own_keys = rotate(
        (key_lin + key_bias).reshape(suffixes, SL, kv_heads, width), cosine, sine
    ).astype(jnp.bfloat16)
    own_keys = own_keys.reshape(suffixes, SL, kv_heads * width)
    own_values = (
        (value_lin + value_bias).astype(jnp.bfloat16).reshape(suffixes, SL, kv_heads * width)
    )
    causal = jnp.arange(SL, dtype=jnp.int32)[None, :] <= jnp.arange(SL, dtype=jnp.int32)[:, None]
    own_part = jax.vmap(partial_attend, in_axes=(0, 0, 0, None))(
        queries, own_keys, own_values, causal
    )
    documents = lax.axis_size("fsdp")
    slots = documents * CAP
    doc_length = key_cache.shape[1]
    order = jnp.arange(suffixes, dtype=jnp.int32)
    earlier = (source_doc[None, :] == source_doc[:, None]) & (order[None, :] < order[:, None])
    ranking = jnp.sum(earlier.astype(jnp.int32), axis=1)
    slot_of = source_doc * CAP + ranking
    matches = slot_of[None, :] == jnp.arange(slots, dtype=jnp.int32)[:, None]
    holder = jnp.sum(jnp.where(matches, order[None, :], 0), axis=1)
    occupied = jnp.any(matches, axis=1)
    slot_length = jnp.where(occupied, jnp.take(prefix_len, holder, axis=0), 0)
    slot_mask = (jnp.arange(doc_length, dtype=jnp.int32)[None, :] < slot_length[:, None]).astype(
        jnp.bfloat16
    )
    slot_queries = jnp.take(queries, holder, axis=0)
    initial = (
        jnp.zeros((suffixes, SL, q_heads * width), jnp.float32),
        jnp.zeros((suffixes, SL, q_heads), jnp.float32),
        jnp.zeros((suffixes, SL, q_heads), jnp.float32),
    )
    key_piece = lax.all_gather(key_cache, "fsdp", axis=0, tiled=True)
    value_piece = lax.all_gather(value_cache, "fsdp", axis=0, tiled=True)
    count = key_piece.shape[0]

    def one_document(item):
        doc_queries, doc_masks, doc_keys, doc_values = item
        live = jnp.broadcast_to(doc_masks[:, None, :] > 0, (CAP, SL, doc_masks.shape[-1]))
        return jax.vmap(partial_attend, in_axes=(0, None, None, 0))(
            doc_queries, doc_keys, doc_values, live
        )

    results = lax.map(
        one_document,
        (
            slot_queries.reshape((count, CAP) + slot_queries.shape[1:]),
            slot_mask.reshape(count, CAP, doc_length),
            key_piece,
            value_piece,
        ),
    )
    results = tuple((part.reshape((count * CAP,) + part.shape[2:]) for part in results))
    inside = (slot_of >= 0) & (slot_of < count * CAP)
    chosen = jnp.clip(slot_of, 0, count * CAP - 1)
    gathered_part = tuple(
        (
            jnp.where(inside[:, None, None], jnp.take(fresh, chosen, axis=0), older)
            for older, fresh in zip(initial, results)
        )
    )
    prefix_normed, prefix_lse = settle(gathered_part)
    attention = combine(prefix_normed, prefix_lse, own_part)
    return attention.reshape(suffixes * SL, q_heads * width)


def solution(mesh):
    in_specs = (
        P("fsdp", "corpus"),
        P(),
        P("fsdp", "corpus"),
        P("fsdp", "corpus"),
        P("fsdp", "corpus"),
        P("corpus"),
        P("corpus"),
        P("corpus"),
        P("fsdp", None, "corpus"),
        P("fsdp", None, "corpus"),
        P("fsdp"),
        P("fsdp"),
    )
    out_specs = P("fsdp", "corpus")
    return jax.shard_map(shards, mesh=mesh, in_specs=in_specs, out_specs=out_specs, check_vma=False)
```

profile of v0, /device:TPU:0, one launch (start us, length us, event | category | flops | bytes accessed | tf_op | source)
XLA Modules:
  0.0 685.7 jit_solution(6007420988527938023)
XLA Ops:
  15.4 31.9 %all-gather.11.cloned.1.call-done = bf16[256,4096]{1,0:T(8,128)(2,1)} async-done(((bf16[256,1024]{1,0:T(8,128)(2,1)}), bf16[256,4096]{1,0:T(8,128)(2,1)}) %all-gather.11.cloned.1.call-update) | async-done | bytes 2097168 | tf_op jit(solution)/shard_map/all_gather | solution.py:97
  47.3 2.2 fusion.13
  49.5 28.5 %all-gather.15.cloned.1.call-done = bf16[4096,256]{1,0:T(8,128)(2,1)} async-done(((bf16[512,256]{1,0:T(8,128)(2,1)}), bf16[4096,256]{1,0:T(8,128)(2,1)}) %all-gather.15.cloned.1.call-update) | async-done | bytes 2097168 | tf_op jit(solution)/shard_map/all_gather | solution.py:106
  78.0 2.4 convolution_add_fusion.2
  80.5 27.7 %all-gather.17.cloned.1.call-done = bf16[4096,256]{1,0:T(8,128)(2,1)} async-done(((bf16[512,256]{1,0:T(8,128)(2,1)}), bf16[4096,256]{1,0:T(8,128)(2,1)}) %all-gather.17.cloned.1.call-update) | async-done | bytes 2097168 | tf_op jit(solution)/shard_map/all_gather | solution.py:111
  108.2 2.4 fusion.27
  110.8 149.5 %all-gather.13.cloned.1.call-done = bf16[4096,2048]{1,0:T(8,128)(2,1)} async-done(((bf16[512,2048]{1,0:T(8,128)(2,1)}), bf16[4096,2048]{1,0:T(8,128)(2,1)}) %all-gather.13.cloned.1.call-update) | async-done | bytes 16777232 | tf_op jit(solution)/shard_map/all_gather | solution.py:101
  260.3 8.2 %fusion.26 = f32[32,8,16,128]{3,1,2,0:T(8,128)S(1)} fusion(bf16[4096,2048]{1,0:T(8,128)(2,1)} %all-gather.13.cloned.1.call-done, f32[2048]{0:T(1024)S(1)} %copy-done.18, bf16[256,4096]{1,0:T(8,128)(2,1)S(1)} %copy-done.7, f32[4096]{0:T(1024)S(1)} %copy-done.17, f32[256]{0:T(256)S(1)} %add_rsqrt_fusion), kind=kOutput, calls=%fused_computation.52 | convolution fusion | flops 4299685888 | bytes 20997120 | tf_op jit(solution)/shard_map/dot_general | solution.py:99
  272.3 1.6 fusion.56
  275.3 2.5 copy.105
  277.8 2.7 reshape.216
  280.5 3.0 fusion.20
  283.5 3.0 gather_fusion.1
  287.0 4.6 broadcast_select_fusion
  291.7 50.4 %all-gather.9.cloned.1.call-done = bf16[8,2048,256]{2,1,0:T(8,128)(2,1)} async-done(((bf16[1,2048,256]{2,1,0:T(8,128)(2,1)}), bf16[8,2048,256]{2,1,0:T(8,128)(2,1)}) %all-gather.9.cloned.1.call-update) | async-done | bytes 8388624 | tf_op jit(solution)/shard_map/all_gather | solution.py:156
  342.1 82.1 %all-gather.7.cloned.1.call-done = bf16[8,2048,256]{2,1,0:T(8,128)(2,1)} async-done(((bf16[1,2048,256]{2,1,0:T(8,128)(2,1)}), bf16[8,2048,256]{2,1,0:T(8,128)(2,1)}) %all-gather.7.cloned.1.call-update) | async-done | bytes 8388624 | tf_op jit(solution)/shard_map/all_gather | solution.py:157
  424.2 241.4 %while.14 = (s32[]{:T(128)}, f32[8,2,64,2048]{3,2,1,0:T(8,128)}, f32[8,2,64,16]{2,3,1,0:T(8,128)S(1)}, f32[8,2,64,16]{2,3,1,0:T(8,128)S(1)}, bf16[8,2048,256]{2,...) while((s32[]{:T(128)}, f32[8,2,64,2048]{3,2,1,0:T(8,128)}, ...), condition=%wide.region_7.8_spmd, body=%wide.region_4.0_spmd.sunk | while | flops 2193620992 | bytes 74047632 | solution.py:167
  428.5 1.4 copy.160
  429.9 7.1 %fusion.71 = (f32[2,64,2,8]{1,3,0,2:T(8,128)S(1)}, f32[2,2048,2,64,8]{1,3,4,2,0:T(8,128)}) fusion(pred[2,2048]{1,0:T(4,128)(4,1)S(1)} %compare_bitcast_fusion.2, bf16[2048,2,128,1,1]{0,2,4,3,1:T(8,128)(2,1)S(1)} %bitcast.138, bf16[2,64,2,8,128]{4,3,2,1,0:T(8,128)(2,1)S(1)} %dynamic-slice_bitcast_fusion.2), kind=kOutput, calls=%fused_computation.9.clone.1 | convolution fusion | flops 1086322688 | bytes 18362368 | tf_op jit(solution)/shard_map/while/body/eval_jaxpr/vmap(tkgd,lkd->tkgl)/dot_general | solution.py:42
  437.1 7.6 %fusion.72 = f32[2,64,2,8,128]{4,1,3,0,2:T(8,128)S(1)} fusion(bf16[2048,2,128,1,1]{0,2,4,3,1:T(8,128)(2,1)S(1)} %bitcast.142, f32[2,2048,2,64,8]{1,3,4,2,0:T(8,128)} %get-tuple-element.168, f32[2,64,2,8]{1,3,0,2:T(8,128)S(1)} %get-tuple-element.169, pred[2,2048]{1,0:T(4,128)(4,1)S(1)} %compare_bitcast_fusion.2), kind=kOutput, calls=%fused_computation.12.clone.1 | convolution fusion | flops 1090519040 | bytes 18886656 | tf_op jit(solution)/shard_map/while/body/eval_jaxpr/vmap(tkgl,lkd->tkgd)/dot_general | solution.py:51
  444.6 7.8 %fusion.73 = f32[2,64,2,8]{1,3,0,2:T(8,128)S(1)} fusion(f32[2,2048,2,64,8]{1,3,4,2,0:T(8,128)} %get-tuple-element.168, f32[2,64,2,8]{1,3,0,2:T(8,128)S(1)} %get-tuple-element.169, pred[2,2048]{1,0:T(4,128)(4,1)S(1)} %compare_bitcast_fusion.2), kind=kLoop, calls=%fused_computation.7.clone.1 | loop fusion | flops 16775168 | bytes 16797696 | tf_op jit(solution)/shard_map/while/body/eval_jaxpr/vmap()/reduce_sum | solution.py:48
  460.1 7.1 %fusion.71 = (f32[2,64,2,8]{1,3,0,2:T(8,128)S(1)}, f32[2,2048,2,64,8]{1,3,4,2,0:T(8,128)}) fusion(pred[2,2048]{1,0:T(4,128)(4,1)S(1)} %compare_bitcast_fusion.2, bf16[2048,2,128,1,1]{0,2,4,3,1:T(8,128)(2,1)S(1)} %bitcast.138, bf16[2,64,2,8,128]{4,3,2,1,0:T(8,128)(2,1)S(1)} %dynamic-slice_bitcast_fusion.2), kind=kOutput, calls=%fused_computation.9.clone.1 | convolution fusion | flops 1086322688 | bytes 18362368 | tf_op jit(solution)/shard_map/while/body/eval_jaxpr/vmap(tkgd,lkd->tkgl)/dot_general | solution.py:42
  467.2 7.6 %fusion.72 = f32[2,64,2,8,128]{4,1,3,0,2:T(8,128)S(1)} fusion(bf16[2048,2,128,1,1]{0,2,4,3,1:T(8,128)(2,1)S(1)} %bitcast.142, f32[2,2048,2,64,8]{1,3,4,2,0:T(8,128)} %get-tuple-element.168, f32[2,64,2,8]{1,3,0,2:T(8,128)S(1)} %get-tuple-element.169, pred[2,2048]{1,0:T(4,128)(4,1)S(1)} %compare_bitcast_fusion.2), kind=kOutput, calls=%fused_computation.12.clone.1 | convolution fusion | flops 1090519040 | bytes 18886656 | tf_op jit(solution)/shard_map/while/body/eval_jaxpr/vmap(tkgl,lkd->tkgd)/dot_general | solution.py:51
  474.8 7.8 %fusion.73 = f32[2,64,2,8]{1,3,0,2:T(8,128)S(1)} fusion(f32[2,2048,2,64,8]{1,3,4,2,0:T(8,128)} %get-tuple-element.168, f32[2,64,2,8]{1,3,0,2:T(8,128)S(1)} %get-tuple-element.169, pred[2,2048]{1,0:T(4,128)(4,1)S(1)} %compare_bitcast_fusion.2), kind=kLoop, calls=%fused_computation.7.clone.1 | loop fusion | flops 16775168 | bytes 16797696 | tf_op jit(solution)/shard_map/while/body/eval_jaxpr/vmap()/reduce_sum | solution.py:48
  488.8 1.4 copy.160
  490.3 7.1 %fusion.71 = (f32[2,64,2,8]{1,3,0,2:T(8,128)S(1)}, f32[2,2048,2,64,8]{1,3,4,2,0:T(8,128)}) fusion(pred[2,2048]{1,0:T(4,128)(4,1)S(1)} %compare_bitcast_fusion.2, bf16[2048,2,128,1,1]{0,2,4,3,1:T(8,128)(2,1)S(1)} %bitcast.138, bf16[2,64,2,8,128]{4,3,2,1,0:T(8,128)(2,1)S(1)} %dynamic-slice_bitcast_fusion.2), kind=kOutput, calls=%fused_computation.9.clone.1 | convolution fusion | flops 1086322688 | bytes 18362368 | tf_op jit(solution)/shard_map/while/body/eval_jaxpr/vmap(tkgd,lkd->tkgl)/dot_general | solution.py:42
  497.4 7.6 %fusion.72 = f32[2,64,2,8,128]{4,1,3,0,2:T(8,128)S(1)} fusion(bf16[2048,2,128,1,1]{0,2,4,3,1:T(8,128)(2,1)S(1)} %bitcast.142, f32[2,2048,2,64,8]{1,3,4,2,0:T(8,128)} %get-tuple-element.168, f32[2,64,2,8]{1,3,0,2:T(8,128)S(1)} %get-tuple-element.169, pred[2,2048]{1,0:T(4,128)(4,1)S(1)} %compare_bitcast_fusion.2), kind=kOutput, calls=%fused_computation.12.clone.1 | convolution fusion | flops 1090519040 | bytes 18886656 | tf_op jit(solution)/shard_map/while/body/eval_jaxpr/vmap(tkgl,lkd->tkgd)/dot_general | solution.py:51
  505.0 7.8 %fusion.73 = f32[2,64,2,8]{1,3,0,2:T(8,128)S(1)} fusion(f32[2,2048,2,64,8]{1,3,4,2,0:T(8,128)} %get-tuple-element.168, f32[2,64,2,8]{1,3,0,2:T(8,128)S(1)} %get-tuple-element.169, pred[2,2048]{1,0:T(4,128)(4,1)S(1)} %compare_bitcast_fusion.2), kind=kLoop, calls=%fused_computation.7.clone.1 | loop fusion | flops 16775168 | bytes 16797696 | tf_op jit(solution)/shard_map/while/body/eval_jaxpr/vmap()/reduce_sum | solution.py:48
  519.0 1.4 copy.160
  520.4 7.1 %fusion.71 = (f32[2,64,2,8]{1,3,0,2:T(8,128)S(1)}, f32[2,2048,2,64,8]{1,3,4,2,0:T(8,128)}) fusion(pred[2,2048]{1,0:T(4,128)(4,1)S(1)} %compare_bitcast_fusion.2, bf16[2048,2,128,1,1]{0,2,4,3,1:T(8,128)(2,1)S(1)} %bitcast.138, bf16[2,64,2,8,128]{4,3,2,1,0:T(8,128)(2,1)S(1)} %dynamic-slice_bitcast_fusion.2), kind=kOutput, calls=%fused_computation.9.clone.1 | convolution fusion | flops 1086322688 | bytes 18362368 | tf_op jit(solution)/shard_map/while/body/eval_jaxpr/vmap(tkgd,lkd->tkgl)/dot_general | solution.py:42
  527.6 7.6 %fusion.72 = f32[2,64,2,8,128]{4,1,3,0,2:T(8,128)S(1)} fusion(bf16[2048,2,128,1,1]{0,2,4,3,1:T(8,128)(2,1)S(1)} %bitcast.142, f32[2,2048,2,64,8]{1,3,4,2,0:T(8,128)} %get-tuple-element.168, f32[2,64,2,8]{1,3,0,2:T(8,128)S(1)} %get-tuple-element.169, pred[2,2048]{1,0:T(4,128)(4,1)S(1)} %compare_bitcast_fusion.2), kind=kOutput, calls=%fused_computation.12.clone.1 | convolution fusion | flops 1090519040 | bytes 18886656 | tf_op jit(solution)/shard_map/while/body/eval_jaxpr/vmap(tkgl,lkd->tkgd)/dot_general | solution.py:51
  535.1 7.8 %fusion.73 = f32[2,64,2,8]{1,3,0,2:T(8,128)S(1)} fusion(f32[2,2048,2,64,8]{1,3,4,2,0:T(8,128)} %get-tuple-element.168, f32[2,64,2,8]{1,3,0,2:T(8,128)S(1)} %get-tuple-element.169, pred[2,2048]{1,0:T(4,128)(4,1)S(1)} %compare_bitcast_fusion.2), kind=kLoop, calls=%fused_computation.7.clone.1 | loop fusion | flops 16775168 | bytes 16797696 | tf_op jit(solution)/shard_map/while/body/eval_jaxpr/vmap()/reduce_sum | solution.py:48
  550.6 7.1 %fusion.71 = (f32[2,64,2,8]{1,3,0,2:T(8,128)S(1)}, f32[2,2048,2,64,8]{1,3,4,2,0:T(8,128)}) fusion(pred[2,2048]{1,0:T(4,128)(4,1)S(1)} %compare_bitcast_fusion.2, bf16[2048,2,128,1,1]{0,2,4,3,1:T(8,128)(2,1)S(1)} %bitcast.138, bf16[2,64,2,8,128]{4,3,2,1,0:T(8,128)(2,1)S(1)} %dynamic-slice_bitcast_fusion.2), kind=kOutput, calls=%fused_computation.9.clone.1 | convolution fusion | flops 1086322688 | bytes 18362368 | tf_op jit(solution)/shard_map/while/body/eval_jaxpr/vmap(tkgd,lkd->tkgl)/dot_general | solution.py:42
  557.7 7.6 %fusion.72 = f32[2,64,2,8,128]{4,1,3,0,2:T(8,128)S(1)} fusion(bf16[2048,2,128,1,1]{0,2,4,3,1:T(8,128)(2,1)S(1)} %bitcast.142, f32[2,2048,2,64,8]{1,3,4,2,0:T(8,128)} %get-tuple-element.168, f32[2,64,2,8]{1,3,0,2:T(8,128)S(1)} %get-tuple-element.169, pred[2,2048]{1,0:T(4,128)(4,1)S(1)} %compare_bitcast_fusion.2), kind=kOutput, calls=%fused_computation.12.clone.1 | convolution fusion | flops 1090519040 | bytes 18886656 | tf_op jit(solution)/shard_map/while/body/eval_jaxpr/vmap(tkgl,lkd->tkgd)/dot_general | solution.py:51
  565.3 7.8 %fusion.73 = f32[2,64,2,8]{1,3,0,2:T(8,128)S(1)} fusion(f32[2,2048,2,64,8]{1,3,4,2,0:T(8,128)} %get-tuple-element.168, f32[2,64,2,8]{1,3,0,2:T(8,128)S(1)} %get-tuple-element.169, pred[2,2048]{1,0:T(4,128)(4,1)S(1)} %compare_bitcast_fusion.2), kind=kLoop, calls=%fused_computation.7.clone.1 | loop fusion | flops 16775168 | bytes 16797696 | tf_op jit(solution)/shard_map/while/body/eval_jaxpr/vmap()/reduce_sum | solution.py:48
  579.4 1.4 copy.160
  580.8 7.1 %fusion.71 = (f32[2,64,2,8]{1,3,0,2:T(8,128)S(1)}, f32[2,2048,2,64,8]{1,3,4,2,0:T(8,128)}) fusion(pred[2,2048]{1,0:T(4,128)(4,1)S(1)} %compare_bitcast_fusion.2, bf16[2048,2,128,1,1]{0,2,4,3,1:T(8,128)(2,1)S(1)} %bitcast.138, bf16[2,64,2,8,128]{4,3,2,1,0:T(8,128)(2,1)S(1)} %dynamic-slice_bitcast_fusion.2), kind=kOutput, calls=%fused_computation.9.clone.1 | convolution fusion | flops 1086322688 | bytes 18362368 | tf_op jit(solution)/shard_map/while/body/eval_jaxpr/vmap(tkgd,lkd->tkgl)/dot_general | solution.py:42
  587.9 7.6 %fusion.72 = f32[2,64,2,8,128]{4,1,3,0,2:T(8,128)S(1)} fusion(bf16[2048,2,128,1,1]{0,2,4,3,1:T(8,128)(2,1)S(1)} %bitcast.142, f32[2,2048,2,64,8]{1,3,4,2,0:T(8,128)} %get-tuple-element.168, f32[2,64,2,8]{1,3,0,2:T(8,128)S(1)} %get-tuple-element.169, pred[2,2048]{1,0:T(4,128)(4,1)S(1)} %compare_bitcast_fusion.2), kind=kOutput, calls=%fused_computation.12.clone.1 | convolution fusion | flops 1090519040 | bytes 18886656 | tf_op jit(solution)/shard_map/while/body/eval_jaxpr/vmap(tkgl,lkd->tkgd)/dot_general | solution.py:51
  595.5 7.8 %fusion.73 = f32[2,64,2,8]{1,3,0,2:T(8,128)S(1)} fusion(f32[2,2048,2,64,8]{1,3,4,2,0:T(8,128)} %get-tuple-element.168, f32[2,64,2,8]{1,3,0,2:T(8,128)S(1)} %get-tuple-element.169, pred[2,2048]{1,0:T(4,128)(4,1)S(1)} %compare_bitcast_fusion.2), kind=kLoop, calls=%fused_computation.7.clone.1 | loop fusion | flops 16775168 | bytes 16797696 | tf_op jit(solution)/shard_map/while/body/eval_jaxpr/vmap()/reduce_sum | solution.py:48
  611.0 7.1 %fusion.71 = (f32[2,64,2,8]{1,3,0,2:T(8,128)S(1)}, f32[2,2048,2,64,8]{1,3,4,2,0:T(8,128)}) fusion(pred[2,2048]{1,0:T(4,128)(4,1)S(1)} %compare_bitcast_fusion.2, bf16[2048,2,128,1,1]{0,2,4,3,1:T(8,128)(2,1)S(1)} %bitcast.138, bf16[2,64,2,8,128]{4,3,2,1,0:T(8,128)(2,1)S(1)} %dynamic-slice_bitcast_fusion.2), kind=kOutput, calls=%fused_computation.9.clone.1 | convolution fusion | flops 1086322688 | bytes 18362368 | tf_op jit(solution)/shard_map/while/body/eval_jaxpr/vmap(tkgd,lkd->tkgl)/dot_general | solution.py:42
  618.1 7.6 %fusion.72 = f32[2,64,2,8,128]{4,1,3,0,2:T(8,128)S(1)} fusion(bf16[2048,2,128,1,1]{0,2,4,3,1:T(8,128)(2,1)S(1)} %bitcast.142, f32[2,2048,2,64,8]{1,3,4,2,0:T(8,128)} %get-tuple-element.168, f32[2,64,2,8]{1,3,0,2:T(8,128)S(1)} %get-tuple-element.169, pred[2,2048]{1,0:T(4,128)(4,1)S(1)} %compare_bitcast_fusion.2), kind=kOutput, calls=%fused_computation.12.clone.1 | convolution fusion | flops 1090519040 | bytes 18886656 | tf_op jit(solution)/shard_map/while/body/eval_jaxpr/vmap(tkgl,lkd->tkgd)/dot_general | solution.py:51
  625.7 7.8 %fusion.73 = f32[2,64,2,8]{1,3,0,2:T(8,128)S(1)} fusion(f32[2,2048,2,64,8]{1,3,4,2,0:T(8,128)} %get-tuple-element.168, f32[2,64,2,8]{1,3,0,2:T(8,128)S(1)} %get-tuple-element.169, pred[2,2048]{1,0:T(4,128)(4,1)S(1)} %compare_bitcast_fusion.2), kind=kLoop, calls=%fused_computation.7.clone.1 | loop fusion | flops 16775168 | bytes 16797696 | tf_op jit(solution)/shard_map/while/body/eval_jaxpr/vmap()/reduce_sum | solution.py:48
  639.7 1.4 copy.160
  641.1 7.1 %fusion.71 = (f32[2,64,2,8]{1,3,0,2:T(8,128)S(1)}, f32[2,2048,2,64,8]{1,3,4,2,0:T(8,128)}) fusion(pred[2,2048]{1,0:T(4,128)(4,1)S(1)} %compare_bitcast_fusion.2, bf16[2048,2,128,1,1]{0,2,4,3,1:T(8,128)(2,1)S(1)} %bitcast.138, bf16[2,64,2,8,128]{4,3,2,1,0:T(8,128)(2,1)S(1)} %dynamic-slice_bitcast_fusion.2), kind=kOutput, calls=%fused_computation.9.clone.1 | convolution fusion | flops 1086322688 | bytes 18362368 | tf_op jit(solution)/shard_map/while/body/eval_jaxpr/vmap(tkgd,lkd->tkgl)/dot_general | solution.py:42
  648.2 7.6 %fusion.72 = f32[2,64,2,8,128]{4,1,3,0,2:T(8,128)S(1)} fusion(bf16[2048,2,128,1,1]{0,2,4,3,1:T(8,128)(2,1)S(1)} %bitcast.142, f32[2,2048,2,64,8]{1,3,4,2,0:T(8,128)} %get-tuple-element.168, f32[2,64,2,8]{1,3,0,2:T(8,128)S(1)} %get-tuple-element.169, pred[2,2048]{1,0:T(4,128)(4,1)S(1)} %compare_bitcast_fusion.2), kind=kOutput, calls=%fused_computation.12.clone.1 | convolution fusion | flops 1090519040 | bytes 18886656 | tf_op jit(solution)/shard_map/while/body/eval_jaxpr/vmap(tkgl,lkd->tkgd)/dot_general | solution.py:51
  655.8 7.8 %fusion.73 = f32[2,64,2,8]{1,3,0,2:T(8,128)S(1)} fusion(f32[2,2048,2,64,8]{1,3,4,2,0:T(8,128)} %get-tuple-element.168, f32[2,64,2,8]{1,3,0,2:T(8,128)S(1)} %get-tuple-element.169, pred[2,2048]{1,0:T(4,128)(4,1)S(1)} %compare_bitcast_fusion.2), kind=kLoop, calls=%fused_computation.7.clone.1 | loop fusion | flops 16775168 | bytes 16797696 | tf_op jit(solution)/shard_map/while/body/eval_jaxpr/vmap()/reduce_sum | solution.py:48
  666.2 4.2 gather_fusion.2
  674.5 4.4 fusion.16
  (191 shorter events, 73.0 us)
Async XLA Ops:
  6.5 40.7 %all-gather.11.cloned.1.call-start = ((), (), s32[]{:S(2)}) async-start(), calls=%async_computation.2 | async-start | bytes 2621440 | tf_op jit(solution)/shard_map/all_gather | solution.py:97
  7.3 70.7 %all-gather.15.cloned.1.call-start = ((), (), s32[]{:S(2)}) async-start(), calls=%async_computation.4 | async-start | bytes 2359296 | tf_op jit(solution)/shard_map/all_gather | solution.py:106
  8.0 100.2 %all-gather.17.cloned.1.call-start = ((), (), s32[]{:S(2)}) async-start(), calls=%async_computation.5 | async-start | bytes 2359296 | tf_op jit(solution)/shard_map/all_gather | solution.py:111
  8.7 1.8 copy-start.16
  8.8 4.3 copy-start
  8.8 251.5 %all-gather.13.cloned.1.call-start = ((), (), s32[]{:S(2)}) async-start(), calls=%async_computation.3 | async-start | bytes 18874368 | tf_op jit(solution)/shard_map/all_gather | solution.py:101
  9.3 332.7 %all-gather.9.cloned.1.call-start = ((), (), s32[]{:S(2)}) async-start(), calls=%async_computation.1 | async-start | bytes 9437184 | tf_op jit(solution)/shard_map/all_gather | solution.py:156
  9.9 68.1 %copy-start.17 = (f32[4096]{0:T(1024)S(1)}, f32[4096]{0:T(1024)}, u32[]{:S(2)}) copy-start(f32[4096]{0:T(1024)} %param.17) | copy-start | bytes 49156
  9.9 68.1 %copy-start.19 = (f32[256]{0:T(256)S(1)}, f32[256]{0:T(256)}, u32[]{:S(2)}) copy-start(f32[256]{0:T(256)} %param.22) | copy-start | bytes 3076
  9.9 414.2 %all-gather.7.cloned.1.call-start = ((), (), s32[]{:S(2)}) async-start(), calls=%async_computation | async-start | bytes 9437184 | tf_op jit(solution)/shard_map/all_gather | solution.py:157
  10.8 0.5 copy-start.10
  12.2 3.2 copy-start.14
  47.3 30.7 %copy-start.7 = (bf16[256,4096]{1,0:T(8,128)(2,1)S(1)}, bf16[256,4096]{1,0:T(8,128)(2,1)}, u32[]{:S(2)}) copy-start(bf16[256,4096]{1,0:T(8,128)(2,1)} %all-gather.11.cloned.1.call-done) | copy-start | bytes 6291460
  49.5 58.7 %copy-start.20 = (f32[256]{0:T(256)S(1)}, f32[256]{0:T(256)}, u32[]{:S(2)}) copy-start(f32[256]{0:T(256)} %param.23) | copy-start | bytes 3076
  80.5 179.8 %copy-start.18 = (f32[2048]{0:T(1024)S(1)}, f32[2048]{0:T(1024)}, u32[]{:S(2)}) copy-start(f32[2048]{0:T(1024)} %param.21) | copy-start | bytes 24580
  269.6 1.3 copy-start.4
  269.6 2.0 copy-start.5
  273.9 1.4 copy-start.2
  283.5 3.0 copy-start.3
  287.0 137.1 %copy-start.8 = (f32[8,2,64,16]{2,3,1,0:T(8,128)S(1)}, f32[8,2,64,16]{2,3,1,0:T(8,128)}, u32[]{:S(2)}) copy-start(f32[8,2,64,16]{2,3,1,0:T(8,128)} %custom-call.12) | copy-start | bytes 196612
  287.0 137.1 %copy-start.9 = (f32[8,2,64,16]{2,3,1,0:T(8,128)S(1)}, f32[8,2,64,16]{2,3,1,0:T(8,128)}, u32[]{:S(2)}) copy-start(f32[8,2,64,16]{2,3,1,0:T(8,128)} %custom-call.11) | copy-start | bytes 196612
  429.9 7.1 %copy-start.1 = (bf16[1,2048,256]{1,2,0:T(8,128)(2,1)S(1)}, bf16[1,2048,256]{1,2,0:T(8,128)(2,1)}, u32[]{:S(2)}) copy-start(bf16[1,2048,256]{1,2,0:T(8,128)(2,1)} %copy.160) | copy-start | bytes 3145732 | tf_op jit(solution)/shard_map/while
  460.1 7.1 %copy-start.1 = (bf16[1,2048,256]{1,2,0:T(8,128)(2,1)S(1)}, bf16[1,2048,256]{1,2,0:T(8,128)(2,1)}, u32[]{:S(2)}) copy-start(bf16[1,2048,256]{1,2,0:T(8,128)(2,1)} %copy.160) | copy-start | bytes 3145732 | tf_op jit(solution)/shard_map/while
  490.3 7.1 %copy-start.1 = (bf16[1,2048,256]{1,2,0:T(8,128)(2,1)S(1)}, bf16[1,2048,256]{1,2,0:T(8,128)(2,1)}, u32[]{:S(2)}) copy-start(bf16[1,2048,256]{1,2,0:T(8,128)(2,1)} %copy.160) | copy-start | bytes 3145732 | tf_op jit(solution)/shard_map/while
  520.4 7.1 %copy-start.1 = (bf16[1,2048,256]{1,2,0:T(8,128)(2,1)S(1)}, bf16[1,2048,256]{1,2,0:T(8,128)(2,1)}, u32[]{:S(2)}) copy-start(bf16[1,2048,256]{1,2,0:T(8,128)(2,1)} %copy.160) | copy-start | bytes 3145732 | tf_op jit(solution)/shard_map/while
  550.6 7.1 %copy-start.1 = (bf16[1,2048,256]{1,2,0:T(8,128)(2,1)S(1)}, bf16[1,2048,256]{1,2,0:T(8,128)(2,1)}, u32[]{:S(2)}) copy-start(bf16[1,2048,256]{1,2,0:T(8,128)(2,1)} %copy.160) | copy-start | bytes 3145732 | tf_op jit(solution)/shard_map/while
  580.8 7.1 %copy-start.1 = (bf16[1,2048,256]{1,2,0:T(8,128)(2,1)S(1)}, bf16[1,2048,256]{1,2,0:T(8,128)(2,1)}, u32[]{:S(2)}) copy-start(bf16[1,2048,256]{1,2,0:T(8,128)(2,1)} %copy.160) | copy-start | bytes 3145732 | tf_op jit(solution)/shard_map/while
  611.0 7.1 %copy-start.1 = (bf16[1,2048,256]{1,2,0:T(8,128)(2,1)S(1)}, bf16[1,2048,256]{1,2,0:T(8,128)(2,1)}, u32[]{:S(2)}) copy-start(bf16[1,2048,256]{1,2,0:T(8,128)(2,1)} %copy.160) | copy-start | bytes 3145732 | tf_op jit(solution)/shard_map/while
  641.1 7.1 %copy-start.1 = (bf16[1,2048,256]{1,2,0:T(8,128)(2,1)S(1)}, bf16[1,2048,256]{1,2,0:T(8,128)(2,1)}, u32[]{:S(2)}) copy-start(bf16[1,2048,256]{1,2,0:T(8,128)(2,1)} %copy.160) | copy-start | bytes 3145732 | tf_op jit(solution)/shard_map/while
  666.2 4.9 copy-start.11
  666.2 4.9 copy-start.15
  672.9 1.6 copy-start.6
  672.9 1.6 copy-start.12
  672.9 1.6 copy-start.13
Sparse Core Ops, SparseCore 0:
  9.2 38.0 all-gather.10
  48.8 29.0 all-gather.14
  79.6 28.5 all-gather.16
  109.7 150.5 all-gather.12
  261.7 80.2 all-gather.8
  343.5 80.5 all-gather.6
where the time goes:
time: 687 us; the launch traced here: 686 us
  waiting for transfers between devices  374 us (54%)
  matrix products  133 us (19%)
  local copies, waits for them, and re-layouts  84.7 us (12%)
  other arithmetic  80.2 us (12%)
  between operations  13.9 us (2%)
    all_gather x1, waiting for transfers between devices, shards(): lax.all_gather(w_query, 'fsdp', axis=0, tiled=True)  150 us
    all_gather x1, waiting for transfers between devices, shards(): value_piece = lax.all_gather(value_cache, 'fsdp', axis=0, tiled=True)  82.1 us
    reduce_sum x9, other arithmetic, partial_attend(): total = jnp.sum(weights, axis=-1)  63 us
    dot_general x9, matrix products, partial_attend(): jnp.einsum('tkgl,lkd->tkgd', rounded, value_rows, preferred_element_type=...  61.1 us
    dot_general x9, matrix products, partial_attend(): jnp.einsum('tkgd,lkd->tkgl', grouped, key_rows, preferred_element_type=jn...  58.6 us
    all_gather x1, waiting for transfers between devices, shards(): key_piece = lax.all_gather(key_cache, 'fsdp', axis=0, tiled=True)  50.4 us
    dynamic_slice x32, local copies, waits for them, and re-layouts, shards(): lax.map(one_document, (slot_queries.reshape((count, CAP) + slot_queries.s...  37.3 us
    all_gather x1, waiting for transfers between devices, shards(): full_rows = lax.all_gather(inputs, 'corpus', axis=1, tiled=True)  31.9 us
  transfers between devices with their start and end apart: 6, of which 6 were waited for; matrix products, arithmetic and copies ran while one was open for 6% of the time, Pallas kernels for 0%

commit v1 on v0

--- a/solution.py
+++ b/solution.py
@@ -154,7 +154,12 @@
         jnp.zeros((suffixes, SL, q_heads), jnp.float32),
     )
     key_piece = lax.all_gather(key_cache, "fsdp", axis=0, tiled=True)
-    value_piece = lax.all_gather(value_cache, "fsdp", axis=0, tiled=True)
+    ring = [value_cache]
+    for hop in range(7):
+        ring.append(lax.ppermute(ring[-1], "fsdp", [(dev, (dev + 1) % 8) for dev in range(8)]))
+    value_piece = jnp.roll(
+        jnp.concatenate(ring[::-1], axis=0), (lax.axis_index("fsdp") + 1) * ring[0].shape[0], axis=0
+    )
     count = key_piece.shape[0]
 
     def one_document(item):

time: 687 us -> 585 us (0.85)
  waiting for transfers between devices: 374 us -> 283 us
  local copies, waits for them, and re-layouts: 84.7 us -> 126 us
  matrix products: 133 us -> 104 us
  other arithmetic: 80.2 us -> 55.4 us
    ppermute x0 -> x7, waiting for transfers between devices: none -> 144 us  [shards(): lax.ppermute(ring[-1], 'fsdp', [(dev, (dev + 1) % 8) for dev in range(8)])]
    all_gather x1 -> x0, waiting for transfers between devices: 82.1 us -> none  [shards(): value_piece = lax.all_gather(value_cache, 'fsdp', axis=0, tiled=True)]
    all_gather x1, waiting for transfers between devices: 150 us -> 76 us  [shards(): lax.all_gather(w_query, 'fsdp', axis=0, tiled=True)]
    all_gather x1, waiting for transfers between devices: 31.9 us -> 0.01 us  [shards(): full_rows = lax.all_gather(inputs, 'corpus', axis=1, tiled=True)]
    reduce_sum x9, other arithmetic: 63 us -> 31.2 us  [partial_attend(): total = jnp.sum(weights, axis=-1)]
    dot_general x9, matrix products: 58.6 us -> 26.8 us  [partial_attend(): jnp.einsum('tkgd,lkd->tkgl', grouped, key_rows, preferred_element_type=jn...]
    all_gather x1, waiting for transfers between devices: 28.5 us -> 0.02 us  [shards(): lax.all_gather(w_key, 'fsdp', axis=0, tiled=True)]
    all_gather x1, waiting for transfers between devices: 27.7 us -> 0.01 us  [shards(): lax.all_gather(w_value, 'fsdp', axis=0, tiled=True)]
  transfers between devices with their start and end apart: 6 -> 12, of which waited for: 6 -> 9; matrix products, arithmetic and copies ran while one was open for 6% -> 13% of each run, Pallas kernels for 0% -> 0%
where the time goes in v1:
time: 585 us; the launch traced here: 583 us
  waiting for transfers between devices  283 us (48%)
  local copies, waits for them, and re-layouts  126 us (22%)
  matrix products  104 us (18%)
  other arithmetic  55.4 us (9%)
  between operations  13.6 us (2%)
    ppermute x7, waiting for transfers between devices, shards(): lax.ppermute(ring[-1], 'fsdp', [(dev, (dev + 1) % 8) for dev in range(8)])  144 us
    all_gather x1, waiting for transfers between devices, shards(): lax.all_gather(w_query, 'fsdp', axis=0, tiled=True)  76 us
    dot_general x9, matrix products, partial_attend(): jnp.einsum('tkgl,lkd->tkgd', rounded, value_rows, preferred_element_type=...  61.2 us
    all_gather x1, waiting for transfers between devices, shards(): key_piece = lax.all_gather(key_cache, 'fsdp', axis=0, tiled=True)  59.8 us
    reduce_sum x9, other arithmetic, partial_attend(): total = jnp.sum(weights, axis=-1)  31.2 us
    dot_general x9, matrix products, partial_attend(): jnp.einsum('tkgd,lkd->tkgl', grouped, key_rows, preferred_element_type=jn...  26.8 us
    unnamed x79, local copies, waits for them, and re-layouts  26.7 us
    dynamic_slice x24, local copies, waits for them, and re-layouts, shards(): lax.map(one_document, (slot_queries.reshape((count, CAP) + slot_queries.s...  26.1 us
  transfers between devices with their start and end apart: 12, of which 9 were waited for; matrix products, arithmetic and copies ran while one was open for 13% of the time, Pallas kernels for 0%

profile of v1, /device:TPU:0, one launch (start us, length us, event | category | flops | bytes accessed | tf_op | source)
XLA Modules:
  0.0 583.0 jit_solution(10307119056081364864)
XLA Ops:
  11.1 16.5 %collective-permute-done = bf16[1,2048,256]{1,2,0:T(8,128)(2,1)S(1)} collective-permute-done((bf16[1,2048,256]{1,2,0:T(8,128)(2,1)S(1)}, bf16[1,2048,256]{1,2,0:T(8,128)(2,1)S(1)}, u32[]{:S(2)}, u32[]{:S(2)}) %collective-permute-start) | collective-permute-done | bytes 1048608 | tf_op jit(solution)/shard_map/ppermute | solution.py:159
  27.6 16.0 %collective-permute-done.1 = bf16[1,2048,256]{1,2,0:T(8,128)(2,1)S(1)} collective-permute-done((bf16[1,2048,256]{1,2,0:T(8,128)(2,1)S(1)}, bf16[1,2048,256]{1,2,0:T(8,128)(2,1)S(1)}, u32[]{:S(2)}, u32[]{:S(2)}) %collective-permute-start.1) | collective-permute-done | bytes 1048608 | tf_op jit(solution)/shard_map/ppermute | solution.py:159
  43.6 16.1 %collective-permute-done.2 = bf16[1,2048,256]{1,2,0:T(8,128)(2,1)S(1)} collective-permute-done((bf16[1,2048,256]{1,2,0:T(8,128)(2,1)S(1)}, bf16[1,2048,256]{1,2,0:T(8,128)(2,1)S(1)}, u32[]{:S(2)}, u32[]{:S(2)}) %collective-permute-start.2) | collective-permute-done | bytes 1048608 | tf_op jit(solution)/shard_map/ppermute | solution.py:159
  61.6 27.4 %collective-permute-done.3 = bf16[1,2048,256]{1,2,0:T(8,128)(2,1)S(1)} collective-permute-done((bf16[1,2048,256]{1,2,0:T(8,128)(2,1)S(1)}, bf16[1,2048,256]{1,2,0:T(8,128)(2,1)S(1)}, u32[]{:S(2)}, u32[]{:S(2)}) %collective-permute-start.3) | collective-permute-done | bytes 1048608 | tf_op jit(solution)/shard_map/ppermute | solution.py:159
  90.3 32.2 %collective-permute-done.4 = bf16[1,2048,256]{1,2,0:T(8,128)(2,1)} collective-permute-done((bf16[1,2048,256]{1,2,0:T(8,128)(2,1)S(1)}, bf16[1,2048,256]{1,2,0:T(8,128)(2,1)}, u32[]{:S(2)}, u32[]{:S(2)}) %collective-permute-start.4) | collective-permute-done | bytes 1048608 | tf_op jit(solution)/shard_map/ppermute | solution.py:159
  129.5 9.5 %collective-permute-done.5 = bf16[1,2048,256]{1,2,0:T(8,128)(2,1)} collective-permute-done((bf16[1,2048,256]{1,2,0:T(8,128)(2,1)}, bf16[1,2048,256]{1,2,0:T(8,128)(2,1)}, u32[]{:S(2)}, u32[]{:S(2)}) %collective-permute-start.5) | collective-permute-done | bytes 1048608 | tf_op jit(solution)/shard_map/ppermute | solution.py:159
  139.1 3.7 convolution_add_fusion.2
  144.6 3.8 fusion.27
  152.0 25.8 %collective-permute-done.6 = bf16[1,2048,256]{1,2,0:T(8,128)(2,1)} collective-permute-done((bf16[1,2048,256]{1,2,0:T(8,128)(2,1)}, bf16[1,2048,256]{1,2,0:T(8,128)(2,1)}, u32[]{:S(2)}, u32[]{:S(2)}) %collective-permute-start.6) | collective-permute-done | bytes 1048608 | tf_op jit(solution)/shard_map/ppermute | solution.py:159
  177.8 2.3 constant_dynamic-update-slice_fusion.16
  180.1 2.3 constant_dynamic-update-slice_fusion.15
  182.4 2.3 constant_dynamic-update-slice_fusion.14
  190.2 2.4 constant_dynamic-update-slice_fusion.8
  192.6 2.3 constant_dynamic-update-slice_fusion.7
  202.5 8.5 %constant_dynamic-slice_fusion.2 = bf16[8,2048,256]{1,2,0:T(8,128)(2,1)} fusion(bf16[16,2048,256]{1,2,0:T(8,128)(2,1)} %constant_dynamic-update-slice_fusion.1, s32[]{:T(128)S(6)} %select_n.106), kind=kLoop, calls=%fused_computation.119 | loop fusion | bytes 16777220 | tf_op jit(solution)/shard_map/jit(_roll_dynamic)/dynamic_slice | solution.py:160
  211.0 76.0 %all-gather.10.cloned.1.call-done = bf16[4096,2048]{1,0:T(8,128)(2,1)} async-done(((bf16[512,2048]{1,0:T(8,128)(2,1)}), bf16[4096,2048]{1,0:T(8,128)(2,1)}) %all-gather.10.cloned.1.call-update) | async-done | bytes 16777232 | tf_op jit(solution)/shard_map/all_gather | solution.py:101
  287.1 8.2 %fusion.26 = f32[32,8,16,128]{3,1,2,0:T(8,128)S(1)} fusion(bf16[4096,2048]{1,0:T(8,128)(2,1)} %all-gather.10.cloned.1.call-done, f32[2048]{0:T(1024)S(1)} %copy-done.29, bf16[256,4096]{1,0:T(8,128)(2,1)S(1)} %copy-done.11, f32[4096]{0:T(1024)S(1)} %copy-done.28, f32[256]{0:T(256)S(1)} %add_rsqrt_fusion), kind=kOutput, calls=%fused_computation.52 | convolution fusion | flops 4299685888 | bytes 20997120 | tf_op jit(solution)/shard_map/dot_general | solution.py:99
  301.2 3.1 gather_fusion.1
  304.4 4.7 broadcast_select_fusion
  309.1 59.8 %all-gather.6.cloned.1.call-done = bf16[8,2048,256]{2,1,0:T(8,128)(2,1)} async-done(((bf16[1,2048,256]{2,1,0:T(8,128)(2,1)}), bf16[8,2048,256]{2,1,0:T(8,128)(2,1)}) %all-gather.6.cloned.1.call-update) | async-done | bytes 8388624 | tf_op jit(solution)/shard_map/all_gather | solution.py:156
  368.9 184.8 %while.14 = (s32[]{:T(128)}, f32[8,2,64,2048]{3,2,1,0:T(8,128)}, f32[8,2,64,16]{2,3,1,0:T(8,128)S(1)}, f32[8,2,64,16]{2,3,1,0:T(8,128)S(1)}, bf16[8,2048,256]{1,...) while((s32[]{:T(128)}, f32[8,2,64,2048]{3,2,1,0:T(8,128)}, ...), condition=%wide.region_7.8_spmd, body=%wide.region_4.0_spmd.sunk | while | flops 2193620992 | bytes 134865552 | solution.py:172
  372.8 2.8 fusion.71
  375.6 3.8 fusion.73
  382.7 7.6 %fusion.72 = f32[2,64,2,8,128]{4,1,3,0,2:T(8,128)S(1)} fusion(bf16[2048,2,128,1,1]{0,2,4,3,1:T(8,128)(2,1)S(1)} %bitcast.142, f32[2,2048,2,64,8]{1,3,4,2,0:T(8,128)} %copy-done, f32[2,64,2,8]{1,3,0,2:T(8,128)S(1)} %get-tuple-element.171, pred[2,2048]{1,0:T(4,128)(4,1)S(1)} %compare_bitcast_fusion.2), kind=kOutput, calls=%fused_computation.12.clone.1 | convolution fusion | flops 1090519040 | bytes 18886656 | tf_op jit(solution)/shard_map/while/body/eval_jaxpr/vmap(tkgl,lkd->tkgd)/dot_general | solution.py:51
  395.9 2.8 fusion.71
  398.7 3.8 fusion.73
  405.8 7.6 %fusion.72 = f32[2,64,2,8,128]{4,1,3,0,2:T(8,128)S(1)} fusion(bf16[2048,2,128,1,1]{0,2,4,3,1:T(8,128)(2,1)S(1)} %bitcast.142, f32[2,2048,2,64,8]{1,3,4,2,0:T(8,128)} %copy-done, f32[2,64,2,8]{1,3,0,2:T(8,128)S(1)} %get-tuple-element.171, pred[2,2048]{1,0:T(4,128)(4,1)S(1)} %compare_bitcast_fusion.2), kind=kOutput, calls=%fused_computation.12.clone.1 | convolution fusion | flops 1090519040 | bytes 18886656 | tf_op jit(solution)/shard_map/while/body/eval_jaxpr/vmap(tkgl,lkd->tkgd)/dot_general | solution.py:51
  419.0 2.8 fusion.71
  421.8 3.8 fusion.73
  428.8 7.6 %fusion.72 = f32[2,64,2,8,128]{4,1,3,0,2:T(8,128)S(1)} fusion(bf16[2048,2,128,1,1]{0,2,4,3,1:T(8,128)(2,1)S(1)} %bitcast.142, f32[2,2048,2,64,8]{1,3,4,2,0:T(8,128)} %copy-done, f32[2,64,2,8]{1,3,0,2:T(8,128)S(1)} %get-tuple-element.171, pred[2,2048]{1,0:T(4,128)(4,1)S(1)} %compare_bitcast_fusion.2), kind=kOutput, calls=%fused_computation.12.clone.1 | convolution fusion | flops 1090519040 | bytes 18886656 | tf_op jit(solution)/shard_map/while/body/eval_jaxpr/vmap(tkgl,lkd->tkgd)/dot_general | solution.py:51
  442.0 2.8 fusion.71
  444.8 3.8 fusion.73
  451.9 7.6 %fusion.72 = f32[2,64,2,8,128]{4,1,3,0,2:T(8,128)S(1)} fusion(bf16[2048,2,128,1,1]{0,2,4,3,1:T(8,128)(2,1)S(1)} %bitcast.142, f32[2,2048,2,64,8]{1,3,4,2,0:T(8,128)} %copy-done, f32[2,64,2,8]{1,3,0,2:T(8,128)S(1)} %get-tuple-element.171, pred[2,2048]{1,0:T(4,128)(4,1)S(1)} %compare_bitcast_fusion.2), kind=kOutput, calls=%fused_computation.12.clone.1 | convolution fusion | flops 1090519040 | bytes 18886656 | tf_op jit(solution)/shard_map/while/body/eval_jaxpr/vmap(tkgl,lkd->tkgd)/dot_general | solution.py:51
  465.1 2.8 fusion.71
  467.9 3.8 fusion.73
  475.0 7.6 %fusion.72 = f32[2,64,2,8,128]{4,1,3,0,2:T(8,128)S(1)} fusion(bf16[2048,2,128,1,1]{0,2,4,3,1:T(8,128)(2,1)S(1)} %bitcast.142, f32[2,2048,2,64,8]{1,3,4,2,0:T(8,128)} %copy-done, f32[2,64,2,8]{1,3,0,2:T(8,128)S(1)} %get-tuple-element.171, pred[2,2048]{1,0:T(4,128)(4,1)S(1)} %compare_bitcast_fusion.2), kind=kOutput, calls=%fused_computation.12.clone.1 | convolution fusion | flops 1090519040 | bytes 18886656 | tf_op jit(solution)/shard_map/while/body/eval_jaxpr/vmap(tkgl,lkd->tkgd)/dot_general | solution.py:51
  488.2 2.8 fusion.71
  491.0 3.8 fusion.73
  498.0 7.6 %fusion.72 = f32[2,64,2,8,128]{4,1,3,0,2:T(8,128)S(1)} fusion(bf16[2048,2,128,1,1]{0,2,4,3,1:T(8,128)(2,1)S(1)} %bitcast.142, f32[2,2048,2,64,8]{1,3,4,2,0:T(8,128)} %copy-done, f32[2,64,2,8]{1,3,0,2:T(8,128)S(1)} %get-tuple-element.171, pred[2,2048]{1,0:T(4,128)(4,1)S(1)} %compare_bitcast_fusion.2), kind=kOutput, calls=%fused_computation.12.clone.1 | convolution fusion | flops 1090519040 | bytes 18886656 | tf_op jit(solution)/shard_map/while/body/eval_jaxpr/vmap(tkgl,lkd->tkgd)/dot_general | solution.py:51
  511.2 2.8 fusion.71
  514.0 3.8 fusion.73
  521.1 7.6 %fusion.72 = f32[2,64,2,8,128]{4,1,3,0,2:T(8,128)S(1)} fusion(bf16[2048,2,128,1,1]{0,2,4,3,1:T(8,128)(2,1)S(1)} %bitcast.142, f32[2,2048,2,64,8]{1,3,4,2,0:T(8,128)} %copy-done, f32[2,64,2,8]{1,3,0,2:T(8,128)S(1)} %get-tuple-element.171, pred[2,2048]{1,0:T(4,128)(4,1)S(1)} %compare_bitcast_fusion.2), kind=kOutput, calls=%fused_computation.12.clone.1 | convolution fusion | flops 1090519040 | bytes 18886656 | tf_op jit(solution)/shard_map/while/body/eval_jaxpr/vmap(tkgl,lkd->tkgd)/dot_general | solution.py:51
  534.3 2.8 fusion.71
  537.1 3.8 fusion.73
  544.2 7.6 %fusion.72 = f32[2,64,2,8,128]{4,1,3,0,2:T(8,128)S(1)} fusion(bf16[2048,2,128,1,1]{0,2,4,3,1:T(8,128)(2,1)S(1)} %bitcast.142, f32[2,2048,2,64,8]{1,3,4,2,0:T(8,128)} %copy-done, f32[2,64,2,8]{1,3,0,2:T(8,128)S(1)} %get-tuple-element.171, pred[2,2048]{1,0:T(4,128)(4,1)S(1)} %compare_bitcast_fusion.2), kind=kOutput, calls=%fused_computation.12.clone.1 | convolution fusion | flops 1090519040 | bytes 18886656 | tf_op jit(solution)/shard_map/while/body/eval_jaxpr/vmap(tkgl,lkd->tkgd)/dot_general | solution.py:51
  555.0 4.6 fusion.56
  560.7 5.6 gather_fusion.2
  572.0 4.4 fusion.16
  (233 shorter events, 117.6 us)
Async XLA Ops:
  6.5 3.4 copy-start.13
  6.5 54.8 %copy-start.26 = (s32[4]{0:T(128)S(1)}, s32[4]{0:T(128)}, u32[]{:S(2)}) copy-start(s32[4]{0:T(128)} %param.26) | copy-start | bytes 52
  6.5 83.6 %copy-start.1 = (s32[4]{0:T(128)S(1)}, s32[4]{0:T(128)}, u32[]{:S(2)}) copy-start(s32[4]{0:T(128)} %param.27) | copy-start | bytes 52
  6.5 120.9 %all-gather.8.cloned.1.call-start = ((), (), s32[]{:S(2)}) async-start(), calls=%async_computation.1 | async-start | bytes 2621440 | tf_op jit(solution)/shard_map/all_gather | solution.py:97
  7.3 131.8 %all-gather.12.cloned.1.call-start = ((), (), s32[]{:S(2)}) async-start(), calls=%async_computation.3 | async-start | bytes 2359296 | tf_op jit(solution)/shard_map/all_gather | solution.py:106
  8.0 136.6 %all-gather.14.cloned.1.call-start = ((), (), s32[]{:S(2)}) async-start(), calls=%async_computation.4 | async-start | bytes 2359296 | tf_op jit(solution)/shard_map/all_gather | solution.py:111
  8.7 130.3 %copy-start.27 = (f32[4096]{0:T(1024)S(1)}, f32[4096]{0:T(1024)}, u32[]{:S(2)}) copy-start(f32[4096]{0:T(1024)} %param.17) | copy-start | bytes 49156
  8.8 130.3 %copy-start.30 = (f32[256]{0:T(256)S(1)}, f32[256]{0:T(256)}, u32[]{:S(2)}) copy-start(f32[256]{0:T(256)} %param.22) | copy-start | bytes 3076
  8.8 278.3 %all-gather.10.cloned.1.call-start = ((), (), s32[]{:S(2)}) async-start(), calls=%async_computation.2 | async-start | bytes 18874368 | tf_op jit(solution)/shard_map/all_gather | solution.py:101
  9.3 359.5 %all-gather.6.cloned.1.call-start = ((), (), s32[]{:S(2)}) async-start(), calls=%async_computation | async-start | bytes 9437184 | tf_op jit(solution)/shard_map/all_gather | solution.py:156
  10.6 17.0 %collective-permute-start = (bf16[1,2048,256]{1,2,0:T(8,128)(2,1)S(1)}, bf16[1,2048,256]{1,2,0:T(8,128)(2,1)S(1)}, u32[]{:S(2)}, u32[]{:S(2)}) collective-permute-start(bf16[1,2048,256]{1,2,0:T(8,128)(2,1)S(1)} %copy.99), channel_id=1, source_target_pairs={{0,1},{1,2},{2,3},{3,4},{4,5},{5,6},{6,7},{7,0},{8,9},{9,10},{10,1... | collective-permute-start | bytes 3145736 | tf_op jit(solution)/shard_map/ppermute | solution.py:159
  27.6 16.0 %collective-permute-start.1 = (bf16[1,2048,256]{1,2,0:T(8,128)(2,1)S(1)}, bf16[1,2048,256]{1,2,0:T(8,128)(2,1)S(1)}, u32[]{:S(2)}, u32[]{:S(2)}) collective-permute-start(bf16[1,2048,256]{1,2,0:T(8,128)(2,1)S(1)} %collective-permute-done), channel_id=1, source_target_pairs={{0,1},{1,2},{2,3},{3,4},{4,5},{5,6},{6,7},{7,0},{8,9},{9,10},{10,1... | collective-permute-start | bytes 3145736 | tf_op jit(solution)/shard_map/ppermute | solution.py:159
  43.6 16.1 %collective-permute-start.2 = (bf16[1,2048,256]{1,2,0:T(8,128)(2,1)S(1)}, bf16[1,2048,256]{1,2,0:T(8,128)(2,1)S(1)}, u32[]{:S(2)}, u32[]{:S(2)}) collective-permute-start(bf16[1,2048,256]{1,2,0:T(8,128)(2,1)S(1)} %collective-permute-done.1), channel_id=1, source_target_pairs={{0,1},{1,2},{2,3},{3,4},{4,5},{5,6},{6,7},{7,0},{8,9},{9,10},{10,1... | collective-permute-start | bytes 3145736 | tf_op jit(solution)/shard_map/ppermute | solution.py:159
  60.7 28.3 %collective-permute-start.3 = (bf16[1,2048,256]{1,2,0:T(8,128)(2,1)S(1)}, bf16[1,2048,256]{1,2,0:T(8,128)(2,1)S(1)}, u32[]{:S(2)}, u32[]{:S(2)}) collective-permute-start(bf16[1,2048,256]{1,2,0:T(8,128)(2,1)S(1)} %collective-permute-done.2), channel_id=1, source_target_pairs={{0,1},{1,2},{2,3},{3,4},{4,5},{5,6},{6,7},{7,0},{8,9},{9,10},{10,1... | collective-permute-start | bytes 3145736 | tf_op jit(solution)/shard_map/ppermute | solution.py:159
  61.5 77.6 %copy-start.20 = (pred[4]{0:T(512)(128)(4,1)}, pred[4]{0:T(512)(128)(4,1)S(1)}, u32[]{:S(2)}) copy-start(pred[4]{0:T(512)(128)(4,1)S(1)} %get-tuple-element.96) | copy-start | bytes 16
  90.0 32.6 %collective-permute-start.4 = (bf16[1,2048,256]{1,2,0:T(8,128)(2,1)S(1)}, bf16[1,2048,256]{1,2,0:T(8,128)(2,1)}, u32[]{:S(2)}, u32[]{:S(2)}) collective-permute-start(bf16[1,2048,256]{1,2,0:T(8,128)(2,1)S(1)} %collective-permute-done.3), channel_id=1, source_target_pairs={{0,1},{1,2},{2,3},{3,4},{4,5},{5,6},{6,7},{7,0},{8,9},{9,10},{10,1... | collective-permute-start | bytes 3145736 | tf_op jit(solution)/shard_map/ppermute | solution.py:159
  90.1 48.9 %copy-start.22 = (pred[4]{0:T(512)(128)(4,1)}, pred[4]{0:T(512)(128)(4,1)S(1)}, u32[]{:S(2)}) copy-start(pred[4]{0:T(512)(128)(4,1)S(1)} %get-tuple-element.98) | copy-start | bytes 16
  122.6 16.4 %collective-permute-start.5 = (bf16[1,2048,256]{1,2,0:T(8,128)(2,1)}, bf16[1,2048,256]{1,2,0:T(8,128)(2,1)}, u32[]{:S(2)}, u32[]{:S(2)}) collective-permute-start(bf16[1,2048,256]{1,2,0:T(8,128)(2,1)} %collective-permute-done.4), channel_id=1, source_target_pairs={{0,1},{1,2},{2,3},{3,4},{4,5},{5,6},{6,7},{7,0},{8,9},{9,10},{10,1... | collective-permute-start | bytes 3145736 | tf_op jit(solution)/shard_map/ppermute | solution.py:159
  129.5 15.1 %copy-start.31 = (f32[256]{0:T(256)S(1)}, f32[256]{0:T(256)}, u32[]{:S(2)}) copy-start(f32[256]{0:T(256)} %param.23) | copy-start | bytes 3076
  139.0 38.8 %collective-permute-start.6 = (bf16[1,2048,256]{1,2,0:T(8,128)(2,1)}, bf16[1,2048,256]{1,2,0:T(8,128)(2,1)}, u32[]{:S(2)}, u32[]{:S(2)}) collective-permute-start(bf16[1,2048,256]{1,2,0:T(8,128)(2,1)} %collective-permute-done.5), channel_id=1, source_target_pairs={{0,1},{1,2},{2,3},{3,4},{4,5},{5,6},{6,7},{7,0},{8,9},{9,10},{10,1... | collective-permute-start | bytes 3145736 | tf_op jit(solution)/shard_map/ppermute | solution.py:159
  143.8 36.3 %copy-start.9 = (f32[4,64,2,128]{3,2,1,0:T(2,128)}, f32[4,64,2,128]{3,2,1,0:T(2,128)S(1)}, u32[]{:S(2)}) copy-start(f32[4,64,2,128]{3,2,1,0:T(2,128)S(1)} %reshape.213) | copy-start | bytes 786436
  150.0 34.8 %copy-start.8 = (bf16[1,2048,256]{1,2,0:T(8,128)(2,1)S(1)}, bf16[1,2048,256]{1,2,0:T(8,128)(2,1)}, u32[]{:S(2)}) copy-start(bf16[1,2048,256]{1,2,0:T(8,128)(2,1)} %copy-done.7) | copy-start | bytes 3145732
  152.0 33.8 %copy-start.6 = (bf16[1,2048,256]{1,2,0:T(8,128)(2,1)S(1)}, bf16[1,2048,256]{1,2,0:T(8,128)(2,1)}, u32[]{:S(2)}) copy-start(bf16[1,2048,256]{1,2,0:T(8,128)(2,1)} %copy-done.5) | copy-start | bytes 3145732
  202.5 84.5 %copy-start.11 = (bf16[256,4096]{1,0:T(8,128)(2,1)S(1)}, bf16[256,4096]{1,0:T(8,128)(2,1)}, u32[]{:S(2)}) copy-start(bf16[256,4096]{1,0:T(8,128)(2,1)} %all-gather.8.cloned.1.call-done) | copy-start | bytes 6291460
  202.5 84.5 %copy-start.28 = (f32[4096]{0:T(1024)S(1)}, f32[4096]{0:T(1024)}, u32[]{:S(2)}) copy-start(f32[4096]{0:T(1024)} %param.17) | copy-start | bytes 49156
  202.5 84.5 %copy-start.29 = (f32[2048]{0:T(1024)S(1)}, f32[2048]{0:T(1024)}, u32[]{:S(2)}) copy-start(f32[2048]{0:T(1024)} %param.21) | copy-start | bytes 24580
  295.6 4.8 copy-start.2
  296.4 4.1 copy-start.12
  304.4 64.5 %copy-start.17 = (f32[8,2,64,16]{2,3,1,0:T(8,128)S(1)}, f32[8,2,64,16]{2,3,1,0:T(8,128)}, u32[]{:S(2)}) copy-start(f32[8,2,64,16]{2,3,1,0:T(8,128)} %custom-call.12) | copy-start | bytes 196612
  304.4 64.5 %copy-start.18 = (f32[8,2,64,16]{2,3,1,0:T(8,128)S(1)}, f32[8,2,64,16]{2,3,1,0:T(8,128)}, u32[]{:S(2)}) copy-start(f32[8,2,64,16]{2,3,1,0:T(8,128)} %custom-call.13) | copy-start | bytes 196612
  368.8 186.1 %copy-start.10 = (f32[4,64,2,128]{3,2,1,0:T(2,128)S(1)}, f32[4,64,2,128]{3,2,1,0:T(2,128)}, u32[]{:S(2)}) copy-start(f32[4,64,2,128]{3,2,1,0:T(2,128)} %copy-done.9) | copy-start | bytes 786436
  368.8 186.2 %copy-start.14 = (f32[4,64,2,64]{3,1,2,0:T(8,128)S(1)}, f32[4,64,2,64]{3,1,2,0:T(8,128)}, u32[]{:S(2)}) copy-start(f32[4,64,2,64]{3,1,2,0:T(8,128)} %get-tuple-element.108) | copy-start | bytes 393220
  368.8 186.2 %copy-start.15 = (f32[4,64,2,64]{3,1,2,0:T(8,128)S(1)}, f32[4,64,2,64]{3,1,2,0:T(8,128)}, u32[]{:S(2)}) copy-start(f32[4,64,2,64]{3,1,2,0:T(8,128)} %get-tuple-element.109) | copy-start | bytes 393220
  368.8 186.2 %copy-start.19 = (pred[64,64]{0,1:T(8,128)(4,1)S(1)}, pred[64,64]{0,1:T(8,128)(4,1)}, u32[]{:S(2)}) copy-start(pred[64,64]{0,1:T(8,128)(4,1)} %iota_compare_fusion) | copy-start | bytes 12292
  375.6 5.8 copy-start
  398.7 5.8 copy-start
  421.8 5.8 copy-start
  444.8 5.8 copy-start
  467.9 5.8 copy-start
  490.9 5.8 copy-start
  514.0 5.8 copy-start
  537.1 5.8 copy-start
  555.0 5.2 copy-start.21
  555.0 5.2 copy-start.23
  559.7 6.6 %copy-start.16 = (bf16[4,64,2,128]{3,2,1,0:T(2,128)(2,1)S(1)}, bf16[4,64,2,128]{3,2,1,0:T(2,128)(2,1)}, u32[]{:S(2)}) copy-start(bf16[4,64,2,128]{3,2,1,0:T(2,128)(2,1)} %reshape_reshape.3) | copy-start | bytes 393220
  569.6 2.5 copy-start.4
  569.6 2.5 copy-start.24
  569.6 2.5 copy-start.25
  (3 other events, 4.4 us)
Sparse Core Ops, SparseCore 0:
  9.2 38.0 all-gather.7
  48.9 34.7 all-gather.11
  85.2 39.8 all-gather.13
  126.6 160.3 all-gather.9
  288.5 80.2 all-gather.5
